TPU v7x, 32 devices: a whole 2x2x4 slice. The times are simulated.
32 devices in a mesh: dom: 2 (over x), shard: 16 (over z, y, core).
Axes of the slice: x: 2, y: 2, z: 4, core: 2. Of those that a mesh axis runs over, the one named last changes fastest.
Arguments:
- activations: bfloat16 [4096, 8192], P(('dom', 'shard')), parts along dimension 0, may hold values from -6 to 6
- out_grads: bfloat16 [4096, 28672], P(('dom', 'shard')), parts along dimension 0, may hold values from -6 to 6
- example_ids: int32 [32, 128], P(('dom', 'shard')), parts along dimension 0, may hold values from 0 to 7, never falling along the last dimension, each value on 1 to 32 neighbouring positions
- in_factor: bfloat16 [64, 8192], P(None, 'shard'), may hold values from -0.0625 to 0.0625
- out_factor: bfloat16 [64, 28672], P(None, 'shard'), may hold values from -0.03125 to 0.03125
- query_grads: float32 [128, 4096], P('shard'), may hold values from -6 to 6
- basis_in: float32 [64, 64], replicated, may hold values from -0.75 to 0.75
- basis_out: float32 [64, 64], replicated, may hold values from -0.75 to 0.75
- eigen: float32 [64, 64], replicated, may hold values from 0.5 to 4
Outputs:
- scores: float32 [256, 128], P('dom', 'shard'), parts along dimension 0
There are 2 independent parts, one for each index of `dom`. A program takes and returns all parts, laid end to end along the dimension named above; an argument that names none is the same for every part. Nothing has to cross between parts.
Inputs may be any that keep to these rules, and one draw needn't show every extreme that they name: `example_ids`: in each row (the 128 tokens of one shard) the example numbers never fall, and every number from 0 to 7 covers 1 to 32 tokens.
All inputs are finite; a program needn't handle non-finite values.
Results may differ from a plain program's by a relative error of at most 0.005.
Values may be sent and summed in bfloat16 or wider, within the bound.
A program may use at most 128 MiB of HBM per device.

v0:
```python
import jax
import jax.numpy as jnp
from jax import lax
from jax.sharding import PartitionSpec as P

EX_DEV = 8


def precondition(query_grads, basis_in, basis_out, eigen):
    rank = basis_in.shape[0]
    grads = query_grads.reshape(-1, rank, rank)
    rotated = jnp.einsum(
        "ai,qab,bj->qij", basis_in, grads, basis_out, precision=lax.Precision.HIGHEST
    )
    scaled = rotated / eigen
    restored = jnp.einsum(
        "ia,qab,jb->qij", basis_in, scaled, basis_out, precision=lax.Precision.HIGHEST
    )
    return restored.reshape(grads.shape[0], -1).astype(jnp.bfloat16)


def fold_columns(features, piece):
    return lax.dot_general(
        features, piece, (((1,), (1,)), ((), ())), preferred_element_type=jnp.float32
    )


def on_device(
    activations,
    out_grads,
    example_ids,
    in_factor,
    out_factor,
    query_grads,
    basis_in,
    basis_out,
    eigen,
):
    rank = in_factor.shape[0]
    proj_in = fold_columns(
        activations, lax.all_gather(in_factor, "shard", axis=1, tiled=True)
    ).astype(jnp.bfloat16)
    proj_out = fold_columns(
        out_grads, lax.all_gather(out_factor, "shard", axis=1, tiled=True)
    ).astype(jnp.bfloat16)
    precond = precondition(query_grads, basis_in, basis_out, eigen)
    total_examples = EX_DEV * lax.axis_size("shard")
    global_ids = example_ids[0] + lax.axis_index("shard") * EX_DEV
    query_mats = precond.reshape(-1, rank, rank)
    rows_in = lax.all_gather(proj_in, "shard", axis=0, tiled=True)
    rows_out = lax.all_gather(proj_out, "shard", axis=0, tiled=True)
    owners = lax.all_gather(global_ids, "shard", axis=0, tiled=True)
    turned = jnp.einsum("ti,qij->tqj", rows_in, query_mats, preferred_element_type=jnp.float32)
    per_token = jnp.sum(turned * rows_out.astype(jnp.float32)[:, None, :], axis=2)
    scores = jax.ops.segment_sum(per_token, owners, num_segments=total_examples)
    return scores * 0.00390625


def solution(mesh):
    placed = (
        P(("dom", "shard"), None),
        P(("dom", "shard"), None),
        P(("dom", "shard"), None),
        P(None, "shard"),
        P(None, "shard"),
        P("shard", None),
        P(),
        P(),
        P(),
    )
    return jax.shard_map(
        on_device, mesh=mesh, in_specs=placed, out_specs=P("dom", "shard"), check_vma=False
    )
```

profile of v0, /device:TPU:0, one launch (start us, length us, event | category | flops | bytes accessed | tf_op | source)
XLA Modules:
  0.0 148.1 jit_solution(9690514091207022177)
XLA Ops:
  6.5 0.0 copy-start
  6.5 0.0 all-gather.4.cloned.1.call-start
  6.5 0.7 all-gather.4.cloned.1.call-update
  7.3 0.0 all-gather.6.cloned.1.call-start
  7.3 0.7 all-gather.6.cloned.1.call-update
  8.0 1.0 reshape.9
  9.0 1.2 fusion.4
  10.2 1.1 convolution_divide_fusion
  11.3 1.1 fusion.2
  12.5 1.1 convolution_convert_fusion
  13.6 0.1 copy.22
  13.7 0.7 broadcast_add_fusion
  14.4 23.1 %all-gather = s32[1,2048]{1,0:T(1,128)S(1)} all-gather(s32[1,128]{1,0:T(1,128)S(1)} %broadcast_add_fusion), channel_id=2, replica_groups=mesh['dom'=2,'shard'=16] {'shard'}, dimensions={1}, use_global_device_ids=true | all-gather | bytes 8704 | tf_op jit(solution)/shard_map/all_gather | solution.py:52
  37.5 11.4 %all-gather.4.cloned.1.call-done = bf16[64,8192]{1,0:T(8,128)(2,1)} async-done(((bf16[64,512]{1,0:T(8,128)(2,1)}), bf16[64,8192]{1,0:T(8,128)(2,1)}) %all-gather.4.cloned.1.call-update) | async-done | bytes 1048592 | tf_op jit(solution)/shard_map/all_gather | solution.py:41
  48.9 0.0 copy-done
  48.9 2.1 %convolution_convert_fusion.2 = bf16[128,64]{0,1:T(8,128)(2,1)S(1)} fusion(bf16[128,8192]{1,0:T(8,128)(2,1)S(1)} %copy-done, bf16[64,8192]{1,0:T(8,128)(2,1)} %all-gather.4.cloned.1.call-done), kind=kOutput, calls=%fused_computation.5 | convolution fusion | flops 134225920 | bytes 3162112 | tf_op jit(solution)/shard_map/dot_general | solution.py:23
  51.0 21.0 %all_gather.17 = bf16[2048,64]{0,1:T(8,128)(2,1)S(1)} all-gather(bf16[128,64]{0,1:T(8,128)(2,1)S(1)} %convolution_convert_fusion.2), channel_id=1, replica_groups=mesh['dom'=2,'shard'=16] {'shard'}, dimensions={0}, use_global_device_ids=true | all-gather | bytes 278528 | tf_op jit(solution)/shard_map/all_gather | solution.py:50
  72.0 27.1 %all-gather.6.cloned.1.call-done = bf16[64,28672]{1,0:T(8,128)(2,1)} async-done(((bf16[64,1792]{1,0:T(8,128)(2,1)}), bf16[64,28672]{1,0:T(8,128)(2,1)}) %all-gather.6.cloned.1.call-update) | async-done | bytes 3670032 | tf_op jit(solution)/shard_map/all_gather | solution.py:44
  99.1 6.8 %convolution_convert_fusion.1 = bf16[128,64]{0,1:T(8,128)(2,1)S(1)} fusion(bf16[128,28672]{1,0:T(8,128)(2,1)} %param.10, bf16[64,28672]{1,0:T(8,128)(2,1)} %all-gather.6.cloned.1.call-done), kind=kOutput, calls=%fused_computation.4 | convolution fusion | flops 469770240 | bytes 11026432 | tf_op jit(solution)/shard_map/dot_general | solution.py:23
  105.9 19.5 %all_gather.19 = bf16[2048,64]{0,1:T(8,128)(2,1)S(1)} all-gather(bf16[128,64]{0,1:T(8,128)(2,1)S(1)} %convolution_convert_fusion.1), channel_id=1, replica_groups=mesh['dom'=2,'shard'=16] {'shard'}, dimensions={0}, use_global_device_ids=true | all-gather | bytes 278528 | tf_op jit(solution)/shard_map/all_gather | solution.py:51
  125.4 0.7 multiply_reduce_fusion
  126.1 0.3 copy.23
  126.4 14.1 %scatter_custom_fusion = f32[128,8]{1,0:T(8,128)S(1)} fusion(s32[2048]{0:T(1024)S(1)} %bitcast.27, f32[2048,8]{1,0:T(8,128)S(1)} %copy.23, f32[]{:T(128)} %constant.4.clone.1), kind=kCustom, calls=%fused_computation.12 | custom fusion | flops 16384 | bytes 4100 | tf_op jit(solution)/shard_map/scatter-add | solution.py:55
  140.6 0.6 broadcast_multiply_fusion
  (2 shorter events, 0.1 us)
Async XLA Ops:
  6.5 42.4 %copy-start = (bf16[128,8192]{1,0:T(8,128)(2,1)S(1)}, bf16[128,8192]{1,0:T(8,128)(2,1)}, u32[]{:S(2)}) copy-start(bf16[128,8192]{1,0:T(8,128)(2,1)} %param.9) | copy-start | bytes 6291460
  6.5 42.4 %all-gather.4.cloned.1.call-start = ((), (), s32[]{:S(2)}) async-start(), calls=%async_computation | async-start | bytes 1114112 | tf_op jit(solution)/shard_map/all_gather | solution.py:41
  7.3 91.9 %all-gather.6.cloned.1.call-start = ((), (), s32[]{:S(2)}) async-start(), calls=%async_computation.1 | async-start | bytes 3899392 | tf_op jit(solution)/shard_map/all_gather | solution.py:44
Sparse Core Ops, SparseCore 0:
  9.5 39.3 all-gather.3
  51.1 47.9 all-gather.5
where the time goes:
time: 149 us; the launch traced here: 148 us
  blocking collectives  63.6 us (43%)
  waiting for transfers between devices  39.9 us (27%)
  other arithmetic  15.4 us (10%)
  matrix products  14.1 us (9%)
  between operations  13.5 us (9%)
  local copies, waits for them, and re-layouts  1.52 us (1%)
    all_gather x1, waiting for transfers between devices, on_device(): lax.all_gather(out_factor, 'shard', axis=1, tiled=True)  27.1 us
    all_gather x1, blocking collectives, on_device(): owners = lax.all_gather(global_ids, 'shard', axis=0, tiled=True)  23.1 us
    all_gather x1, blocking collectives, on_device(): rows_in = lax.all_gather(proj_in, 'shard', axis=0, tiled=True)  21 us
    all_gather x1, blocking collectives, on_device(): rows_out = lax.all_gather(proj_out, 'shard', axis=0, tiled=True)  19.5 us
    scatter-add x1, other arithmetic, on_device(): scores = jax.ops.segment_sum(per_token, owners, num_segments=total_examples)  14.1 us
    all_gather x1, waiting for transfers between devices, on_device(): lax.all_gather(in_factor, 'shard', axis=1, tiled=True)  11.4 us
    dot_general x2, matrix products, fold_columns(): lax.dot_general(features, piece, (((1,), (1,)), ((), ())), preferred_elem...  8.84 us
  transfers between devices with their start and end apart: 2, of which 2 were waited for; matrix products, arithmetic and copies ran while one was open for 6% of the time, Pallas kernels for 0%

commit v1 on v0

--- a/solution.py
+++ b/solution.py
@@ -1,31 +1,38 @@
+import functools
+
 import jax
 import jax.numpy as jnp
 from jax import lax
+from jax.experimental import pallas as pl
+from jax.experimental.pallas import tpu as pltpu
 from jax.sharding import PartitionSpec as P
 
 EX_DEV = 8
+MESH = pl.DeviceIdType.MESH
+HIGHEST = lax.Precision.HIGHEST
+NT = (((1,), (1,)), ((), ()))
+SCALE = 0.00390625
+IDS = 16
 
 
 def precondition(query_grads, basis_in, basis_out, eigen):
     rank = basis_in.shape[0]
     grads = query_grads.reshape(-1, rank, rank)
     rotated = jnp.einsum(
-        "ai,qab,bj->qij", basis_in, grads, basis_out, precision=lax.Precision.HIGHEST
+        "ai,qab,bj->qij", basis_in, grads, basis_out, precision=HIGHEST
     )
     scaled = rotated / eigen
     restored = jnp.einsum(
-        "ia,qab,jb->qij", basis_in, scaled, basis_out, precision=lax.Precision.HIGHEST
+        "ia,qab,jb->qij", basis_in, scaled, basis_out, precision=HIGHEST
     )
     return restored.reshape(grads.shape[0], -1).astype(jnp.bfloat16)
 
 
 def fold_columns(features, piece):
-    return lax.dot_general(
-        features, piece, (((1,), (1,)), ((), ())), preferred_element_type=jnp.float32
-    )
-
-
-def on_device(
+    return lax.dot_general(features, piece, NT, preferred_element_type=jnp.float32)
+
+
+def with_collectives(
     activations,
     out_grads,
     example_ids,
@@ -53,7 +60,365 @@
     turned = jnp.einsum("ti,qij->tqj", rows_in, query_mats, preferred_element_type=jnp.float32)
     per_token = jnp.sum(turned * rows_out.astype(jnp.float32)[:, None, :], axis=2)
     scores = jax.ops.segment_sum(per_token, owners, num_segments=total_examples)
-    return scores * 0.00390625
+    return scores * SCALE
+
+
+def pick(value, table):
+    found = jnp.int32(table[0])
+    for key in range(1, len(table)):
+        found = jnp.where(value == key, jnp.int32(table[key]), found)
+    return found
+
+
+def kernel(
+    lines,
+    acts_hbm,
+    grads_hbm,
+    ids_ref,
+    fin_hbm,
+    fout_hbm,
+    query_ref,
+    bin_ref,
+    bout_ref,
+    eig_ref,
+    out_ref,
+    acts,
+    grads,
+    fin,
+    fout,
+    rin,
+    rout,
+    acc_in,
+    acc_out,
+    turned,
+    mats,
+    blocks,
+    wide,
+    load_sem,
+    send_fin,
+    send_fout,
+    send_rin,
+    send_rout,
+    recv_fin,
+    recv_fout,
+    recv_rin,
+    recv_rout,
+):
+    x = lax.axis_index("dom")
+    s = lax.axis_index("shard")
+    z, y, c = s // 4, (s // 2) % 2, s % 2
+    rank = fin.shape[1]
+    half = rank // 2
+    quarter = rank // 4
+    n_query = query_ref.shape[0]
+
+    def place(zz, yy, cc):
+        return (zz * 2 + yy) * 2 + cc
+
+    up = jnp.minimum(z + 1, lines - 1)
+    down = jnp.maximum(z - 1, 0)
+    has_up, has_down = z < lines - 1, z > 0
+    dev_up, dev_down = (x, place(up, y, c)), (x, place(down, y, c))
+    dev_y, dev_x, dev_core = (x, place(z, 1 - y, c)), (1 - x, s), (x, place(z, y, 1 - c))
+
+    loads = [
+        pltpu.make_async_copy(fin_hbm, fin.at[s], load_sem.at[0]),
+        pltpu.make_async_copy(fout_hbm, fout.at[s], load_sem.at[1]),
+        pltpu.make_async_copy(acts_hbm, acts, load_sem.at[2]),
+        pltpu.make_async_copy(grads_hbm, grads, load_sem.at[3]),
+    ]
+    for load in loads:
+        load.start()
+
+    barrier = pltpu.get_barrier_semaphore()
+
+    def greet(dev):
+        pl.semaphore_signal(barrier, inc=1, device_id=dev, device_id_type=MESH)
+
+    @pl.when(has_up)
+    def _():
+        greet(dev_up)
+
+    @pl.when(has_down)
+    def _():
+        greet(dev_down)
+
+    greet(dev_y)
+    greet(dev_x)
+    greet(dev_core)
+    pl.semaphore_wait(
+        barrier, 3 + jnp.where(has_up, 1, 0) + jnp.where(has_down, 1, 0)
+    )
+
+    stores = (fin, fout, rin, rout)
+    sends = (send_fin, send_fout, send_rin, send_rout)
+    recvs = (recv_fin, recv_fout, recv_rin, recv_rout)
+    pending = []
+
+    def block(f, g):
+        if f >= 2:
+            return 0, 0, stores[f].shape[1]
+        if g == "native":
+            return x, pl.multiple_of(x * quarter, quarter), quarter
+        if g == "cross":
+            return 1 - x, pl.multiple_of((1 - x) * quarter, quarter), quarter
+        return 2, half, half
+
+    def copy(f, g, p, kind, dev):
+        slot, start, size = block(f, g)
+        ref = stores[f].at[p, pl.ds(start, size)]
+        return pltpu.make_async_remote_copy(
+            src_ref=ref,
+            dst_ref=ref,
+            send_sem=sends[f].at[kind, slot, p],
+            recv_sem=recvs[f].at[slot, p],
+            device_id=dev,
+            device_id_type=MESH,
+        )
+
+    def send(f, g, p, kind, dev, cond=None):
+        make = functools.partial(copy, f, g, p, kind, dev)
+        if cond is None:
+            make().start()
+        else:
+
+            @pl.when(cond)
+            def _():
+                make().start()
+
+        pending.append((cond, make))
+
+    def arrive(f, g, p):
+        copy(f, g, p, 0, dev_core).wait_recv()
+
+    def along(f, g, p, zz=None):
+        if zz is None:
+            send(f, g, p, 0, dev_up, has_up)
+            send(f, g, p, 1, dev_down, has_down)
+            return
+        from_below = zz < z
+        dev = (x, jnp.where(from_below, dev_up[1], dev_down[1]))
+        cond = jnp.where(from_below, z + 1, lines - z) < lines
+        send(f, g, p, 0, dev, cond)
+
+    def yz_first(f, g):
+        return f == 0 and g == "rest"
+
+    def own(f):
+        for g in ("native", "rest") if f < 2 else ("all",):
+            along(f, g, s)
+            send(f, g, s, 2, dev_y)
+        for g in ("native", "cross", "rest") if f < 2 else ("all",):
+            send(f, g, s, 4, dev_core)
+
+    near = [
+        sorted([w for w in range(lines) if w != v], key=lambda w: (abs(w - v), w))
+        for v in range(lines)
+    ]
+    others = [pick(z, [near[v][k] for v in range(lines)]) for k in range(lines - 1)]
+    route = [(None, True)]
+    for far in others:
+        route += [(far, False), (far, True)]
+
+    def spot(k, cc):
+        far, turn = route[k]
+        return place(z if far is None else far, 1 - y if turn else y, cc)
+
+    def native(f, k):
+        far, turn = route[k]
+        p = spot(k, c)
+        for g in ("native", "rest") if f < 2 else ("all",):
+            arrive(f, g, p)
+            if yz_first(f, g):
+                along(f, g, p, far)
+            elif not turn:
+                along(f, g, p, far)
+                send(f, g, p, 2, dev_y)
+            if g == "native":
+                send(f, g, p, 3, dev_x)
+            send(f, g, p, 4, dev_core)
+
+    def fold(f, p):
+        xs, acc = ((acts, acc_in), (grads, acc_out))[f]
+        width = stores[f].shape[2]
+        cols = pl.ds(pl.multiple_of(p * width, 128), width)
+        acc[...] += fold_columns(stores[f][p], xs[:, cols])
+
+    def cross(f, k):
+        p = spot(k, c)
+        arrive(f, "cross", p)
+        send(f, "cross", p, 4, dev_core)
+        fold(f, p)
+
+    def partner(f, k):
+        p = dev_core[1] if k < 0 else spot(k, 1 - c)
+        for g in ("native", "cross", "rest") if f < 2 else ("all",):
+            arrive(f, g, p)
+        if f < 2:
+            fold(f, p)
+
+    def turn_rows(p):
+        turned[p] = jnp.dot(
+            mats[...], rin[p, pl.ds(0, rank), :], preferred_element_type=jnp.float32
+        )
+
+    def finish(p):
+        rows = rout[p].astype(jnp.float32)
+        prod = turned[p].reshape(n_query, rank, rows.shape[1]) * rows[None]
+        per_token = jnp.sum(prod, axis=1)
+        ids = rin[p, pl.ds(rank, IDS), :].astype(jnp.float32)[:EX_DEV]
+        want = lax.broadcasted_iota(jnp.int32, ids.shape, 0).astype(jnp.float32)
+        member = jnp.where(ids == want, 1.0, 0.0).astype(jnp.bfloat16)
+        high = per_token.astype(jnp.bfloat16)
+        low = (per_token - high.astype(jnp.float32)).astype(jnp.bfloat16)
+        total = fold_columns(member, high) + fold_columns(member, low)
+        out_ref[pl.ds(pl.multiple_of(p * EX_DEV, EX_DEV), EX_DEV), :] = total * SCALE
+
+    loads[0].wait()
+    own(0)
+    loads[1].wait()
+    own(1)
+
+    acc_in[...] = jnp.zeros_like(acc_in)
+    acc_out[...] = jnp.zeros_like(acc_out)
+    ids = jnp.broadcast_to(ids_ref[...].astype(jnp.float32), (IDS, ids_ref.shape[1]))
+    rin[s, pl.ds(rank, IDS), :] = ids.astype(jnp.bfloat16)
+
+    for a in range(rank):
+        blocks[a] = query_ref[:, a * rank : (a + 1) * rank]
+    first = jnp.dot(
+        blocks[...].reshape(rank * n_query, rank), bout_ref[...], precision=HIGHEST
+    )
+    blocks[...] = first.reshape(rank, n_query, rank)
+    for q in range(n_query):
+        wide[:, q * rank : (q + 1) * rank] = blocks[:, q, :]
+    rotated = jnp.dot(bin_ref[...].T, wide[...], precision=HIGHEST)
+    wide[...] = rotated / jnp.concatenate([eig_ref[...]] * n_query, axis=1)
+    wide[...] = jnp.dot(bin_ref[...], wide[...], precision=HIGHEST)
+    for q in range(n_query):
+        mats[q * rank : (q + 1) * rank, :] = lax.dot_general(
+            bout_ref[...], wide[:, q * rank : (q + 1) * rank], NT, precision=HIGHEST,
+            preferred_element_type=jnp.float32,
+        ).astype(jnp.bfloat16)
+
+    steps = len(route)
+    order = [(f, k) for f in range(2) for k in range(steps)]
+    lag, slow = 2, 3
+    done_in = None
+    rows_at = None
+    row_step = 0
+    for i in range(len(order) + slow):
+        if i < len(order):
+            native(*order[i])
+        if i == 1:
+            loads[2].wait()
+            fold(0, s)
+            partner(0, -1)
+        if i == steps + 1:
+            loads[3].wait()
+            fold(1, s)
+            partner(1, -1)
+        if 0 <= i - lag < len(order):
+            cross(*order[i - lag])
+        if 0 <= i - slow:
+            partner(*order[i - slow])
+            if order[i - slow] == (0, steps - 1):
+                rin[s, pl.ds(0, rank), :] = acc_in[...].astype(jnp.bfloat16)
+                own(2)
+                turn_rows(s)
+                rows_at = i
+        if rows_at is not None and i > rows_at and row_step < steps:
+            native(2, row_step)
+            turn_rows(spot(row_step, c))
+            row_step += 1
+    rout[s] = acc_out[...].astype(jnp.bfloat16)
+    own(3)
+    while row_step < steps:
+        native(2, row_step)
+        turn_rows(spot(row_step, c))
+        row_step += 1
+    for k in range(-1, steps):
+        partner(2, k)
+        turn_rows(dev_core[1] if k < 0 else spot(k, 1 - c))
+    finish(s)
+    partner(3, -1)
+    finish(dev_core[1])
+    for k in range(steps):
+        native(3, k)
+        finish(spot(k, c))
+    for k in range(steps):
+        partner(3, k)
+        finish(spot(k, 1 - c))
+
+    for cond, make in pending:
+        if cond is None:
+            make().wait_send()
+        else:
+
+            @pl.when(cond)
+            def _(make=make):
+                make().wait_send()
+
+
+def in_one_kernel(
+    activations,
+    out_grads,
+    example_ids,
+    in_factor,
+    out_factor,
+    query_grads,
+    basis_in,
+    basis_out,
+    eigen,
+):
+    n = lax.axis_size("shard")
+    rank = in_factor.shape[0]
+    tokens = activations.shape[0]
+    n_query = query_grads.shape[0]
+    bf16, f32 = jnp.bfloat16, jnp.float32
+    hbm = pl.BlockSpec(memory_space=pl.ANY)
+    vmem = pl.BlockSpec(memory_space=pltpu.VMEM)
+    dma = pltpu.SemaphoreType.DMA
+    return pl.pallas_call(
+        functools.partial(kernel, n // 4),
+        out_shape=jax.ShapeDtypeStruct((n * EX_DEV, n_query), f32),
+        in_specs=[hbm, hbm, vmem, hbm, hbm, vmem, vmem, vmem, vmem],
+        out_specs=vmem,
+        scratch_shapes=[
+            pltpu.VMEM(activations.shape, bf16),
+            pltpu.VMEM(out_grads.shape, bf16),
+            pltpu.VMEM((n,) + in_factor.shape, bf16),
+            pltpu.VMEM((n,) + out_factor.shape, bf16),
+            pltpu.VMEM((n, rank + IDS, tokens), bf16),
+            pltpu.VMEM((n, rank, tokens), bf16),
+            pltpu.VMEM((rank, tokens), f32),
+            pltpu.VMEM((rank, tokens), f32),
+            pltpu.VMEM((n, n_query * rank, tokens), f32),
+            pltpu.VMEM((n_query * rank, rank), bf16),
+            pltpu.VMEM((rank, n_query, rank), f32),
+            pltpu.VMEM((rank, n_query * rank), f32),
+            dma((4,)),
+            dma((5, 3, n)),
+            dma((5, 3, n)),
+            dma((5, 1, n)),
+            dma((5, 1, n)),
+            dma((3, n)),
+            dma((3, n)),
+            dma((1, n)),
+            dma((1, n)),
+        ],
+        compiler_params=pltpu.CompilerParams(collective_id=0, has_side_effects=True),
+    )(
+        activations,
+        out_grads,
+        example_ids,
+        in_factor,
+        out_factor,
+        query_grads,
+        basis_in,
+        basis_out,
+        eigen,
+    )
 
 
 def solution(mesh):
@@ -68,6 +433,11 @@
         P(),
         P(),
     )
+    small = mesh.shape["dom"] == 2 and mesh.shape["shard"] in (8, 16)
     return jax.shard_map(
-        on_device, mesh=mesh, in_specs=placed, out_specs=P("dom", "shard"), check_vma=False
-    )
+        in_one_kernel if small else with_collectives,
+        mesh=mesh,
+        in_specs=placed,
+        out_specs=P("dom", "shard"),
+        check_vma=False,
+    )

time: 149 us -> 72.8 us (0.49)
  Pallas kernels: 0 us -> 71.1 us
  blocking collectives: 63.6 us -> 0 us
  waiting for transfers between devices: 39.9 us -> 0 us
  other arithmetic: 15.4 us -> 0 us
  matrix products: 14.1 us -> 0 us
  between operations: 13.5 us -> 0.01 us
    pallas_call x0 -> x1, Pallas kernels: none -> 71.1 us  [in_one_kernel(): pl.pallas_call(functools.partial(kernel, n // 4), out_shape=jax.ShapeDtyp...]
    all_gather x3 -> x0, blocking collectives: 63.6 us -> none  [the longest x1 23.1 us: on_device(): owners = lax.all_gather(global_ids, 'shard', axis=0, tiled=True)]
    all_gather x2 -> x0, waiting for transfers between devices: 38.5 us -> none  [the longest x1 27.1 us: on_device(): lax.all_gather(out_factor, 'shard', axis=1, tiled=True)]
    scatter-add x1 -> x0, other arithmetic: 14.1 us -> none  [on_device(): scores = jax.ops.segment_sum(per_token, owners, num_segments=total_examples)]
    dot_general x6 -> x0, matrix products: 13.4 us -> none  [the longest x2 8.84 us: fold_columns(): lax.dot_general(features, piece, (((1,), (1,)), ((), ())), preferred_elem...]
    pallas_call x0 -> x1, local copies, waits for them, and re-layouts: none -> 1.5 us  [in_one_kernel(): pl.pallas_call(functools.partial(kernel, n // 4), out_shape=jax.ShapeDtyp...]
  transfers between devices with their start and end apart: 2 -> 0, of which waited for: 2 -> 0; matrix products, arithmetic and copies ran while one was open for 6% -> 0% of each run, Pallas kernels for 0% -> 0%
where the time goes in v1:
time: 72.8 us; the launch traced here: 72.6 us
  Pallas kernels  71.1 us (98%)
  local copies, waits for them, and re-layouts  1.5 us (2%)
    pallas_call x1, Pallas kernels, in_one_kernel(): pl.pallas_call(functools.partial(kernel, n // 4), out_shape=jax.ShapeDtyp...  71.1 us
    pallas_call x1, local copies, waits for them, and re-layouts, in_one_kernel(): pl.pallas_call(functools.partial(kernel, n // 4), out_shape=jax.ShapeDtyp...  1.5 us

profile of v1, /device:TPU:0, one launch (start us, length us, event | category | flops | bytes accessed | tf_op | source)
XLA Modules:
  0.0 72.6 jit_solution(16658053200973952893)
XLA Ops:
  0.0 71.1 %shard_map.91 = f32[128,8]{1,0:T(8,128)} custom-call(bf16[128,8192]{1,0:T(8,128)(2,1)} %acts_hbm.1, bf16[128,28672]{1,0:T(8,128)(2,1)} %grads_hbm.1, s32[1,128]{1,0:T(1,128)} %ids_ref.1, bf16[64,512]{1,0:T(8,128)(2,1)} %fin_hbm.1, bf16[64,1792]{1,0:T(8,128)(2,1)} %fout_hbm.1, f32[8,4096]{1,0:T(8,128)} %query_ref.1, f32[64,64]{1,0:T(8,128)} %bin_ref.1, ...), custom_call_target="tpu_custom_call" | custom-call | tf_op jit(solution)/shard_map/pallas_call | solution.py:382
  71.1 1.5 %copy.10 = f32[128,8]{0,1:T(8,128)} copy(f32[128,8]{1,0:T(8,128)} %shard_map.91) | data formatting | bytes 8192 | tf_op jit(solution)/shard_map/pallas_call | solution.py:382

commit v2 on v1

--- a/solution.py
+++ b/solution.py
@@ -205,10 +205,10 @@
         return f == 0 and g == "rest"
 
     def own(f):
-        for g in ("native", "rest") if f < 2 else ("all",):
+        for g in ("native", "rest"):
             along(f, g, s)
             send(f, g, s, 2, dev_y)
-        for g in ("native", "cross", "rest") if f < 2 else ("all",):
+        for g in ("native", "cross", "rest"):
             send(f, g, s, 4, dev_core)
 
     near = [
@@ -224,10 +224,20 @@
         far, turn = route[k]
         return place(z if far is None else far, 1 - y if turn else y, cc)
 
+    def spread(f):
+        for k in reversed(range(len(route))):
+            send(f, "all", s, k, (x, spot(k, c)))
+        send(f, "all", s, len(route), dev_core)
+
+    def passed(f, k):
+        p = spot(k, c)
+        arrive(f, "all", p)
+        send(f, "all", p, len(route), dev_core)
+
     def native(f, k):
         far, turn = route[k]
         p = spot(k, c)
-        for g in ("native", "rest") if f < 2 else ("all",):
+        for g in ("native", "rest"):
             arrive(f, g, p)
             if yz_first(f, g):
                 along(f, g, p, far)
@@ -252,10 +262,9 @@
 
     def partner(f, k):
         p = dev_core[1] if k < 0 else spot(k, 1 - c)
-        for g in ("native", "cross", "rest") if f < 2 else ("all",):
+        for g in ("native", "cross", "rest"):
             arrive(f, g, p)
-        if f < 2:
-            fold(f, p)
+        fold(f, p)
 
     def turn_rows(p):
         turned[p] = jnp.dot(
@@ -302,52 +311,54 @@
         ).astype(jnp.bfloat16)
 
     steps = len(route)
-    order = [(f, k) for f in range(2) for k in range(steps)]
-    lag, slow = 2, 3
-    done_in = None
-    rows_at = None
-    row_step = 0
-    for i in range(len(order) + slow):
-        if i < len(order):
-            native(*order[i])
-        if i == 1:
-            loads[2].wait()
-            fold(0, s)
-            partner(0, -1)
-        if i == steps + 1:
-            loads[3].wait()
-            fold(1, s)
-            partner(1, -1)
-        if 0 <= i - lag < len(order):
+    lead, lag, slow = 3, 3, 4
+    order = []
+    for k in range(steps + lead):
+        if k < steps:
+            order.append((0, k))
+        if k >= lead:
+            order.append((1, k - lead))
+    fold_own = {2: 0, 6: 1}
+
+    def close(f, k):
+        partner(f, k)
+        if (f, k) == (0, steps - 1):
+            rin[s, pl.ds(0, rank), :] = acc_in[...].astype(jnp.bfloat16)
+            spread(2)
+
+    for i in range(len(order)):
+        native(*order[i])
+        if i in fold_own:
+            f = fold_own[i]
+            loads[2 + f].wait()
+            fold(f, s)
+            partner(f, -1)
+        if i >= lag:
             cross(*order[i - lag])
-        if 0 <= i - slow:
-            partner(*order[i - slow])
-            if order[i - slow] == (0, steps - 1):
-                rin[s, pl.ds(0, rank), :] = acc_in[...].astype(jnp.bfloat16)
-                own(2)
-                turn_rows(s)
-                rows_at = i
-        if rows_at is not None and i > rows_at and row_step < steps:
-            native(2, row_step)
-            turn_rows(spot(row_step, c))
-            row_step += 1
+        if i >= slow:
+            close(*order[i - slow])
+    turn_rows(s)
+    for k in range(steps):
+        passed(2, k)
+        turn_rows(spot(k, c))
+    for i in range(len(order), len(order) + slow):
+        if i - lag < len(order):
+            cross(*order[i - lag])
+        close(*order[i - slow])
     rout[s] = acc_out[...].astype(jnp.bfloat16)
-    own(3)
-    while row_step < steps:
-        native(2, row_step)
-        turn_rows(spot(row_step, c))
-        row_step += 1
+    spread(3)
     for k in range(-1, steps):
-        partner(2, k)
-        turn_rows(dev_core[1] if k < 0 else spot(k, 1 - c))
+        p = dev_core[1] if k < 0 else spot(k, 1 - c)
+        arrive(2, "all", p)
+        turn_rows(p)
     finish(s)
-    partner(3, -1)
+    arrive(3, "all", dev_core[1])
     finish(dev_core[1])
     for k in range(steps):
-        native(3, k)
+        passed(3, k)
         finish(spot(k, c))
     for k in range(steps):
-        partner(3, k)
+        arrive(3, "all", spot(k, 1 - c))
         finish(spot(k, 1 - c))
 
     for cond, make in pending:
@@ -400,8 +411,8 @@
             dma((4,)),
             dma((5, 3, n)),
             dma((5, 3, n)),
-            dma((5, 1, n)),
-            dma((5, 1, n)),
+            dma((n // 2, 1, n)),
+            dma((n // 2, 1, n)),
             dma((3, n)),
             dma((3, n)),
             dma((1, n)),

time: 72.8 us -> 62.2 us (0.85)
  Pallas kernels: 71.1 us -> 60.5 us
    pallas_call x1, Pallas kernels: 71.1 us -> 60.5 us  [in_one_kernel(): pl.pallas_call(functools.partial(kernel, n // 4), out_shape=jax.ShapeDtyp...]
where the time goes in v2:
time: 62.2 us; the launch traced here: 62 us
  Pallas kernels  60.5 us (97%)
  local copies, waits for them, and re-layouts  1.5 us (2%)
    pallas_call x1, Pallas kernels, in_one_kernel(): pl.pallas_call(functools.partial(kernel, n // 4), out_shape=jax.ShapeDtyp...  60.5 us
    pallas_call x1, local copies, waits for them, and re-layouts, in_one_kernel(): pl.pallas_call(functools.partial(kernel, n // 4), out_shape=jax.ShapeDtyp...  1.5 us

profile of v2, /device:TPU:0, one launch (start us, length us, event | category | flops | bytes accessed | tf_op | source)
XLA Modules:
  0.0 62.0 jit_solution(9559690430451375019)
XLA Ops:
  0.0 60.5 %shard_map.91 = f32[128,8]{1,0:T(8,128)} custom-call(bf16[128,8192]{1,0:T(8,128)(2,1)} %acts_hbm.1, bf16[128,28672]{1,0:T(8,128)(2,1)} %grads_hbm.1, s32[1,128]{1,0:T(1,128)} %ids_ref.1, bf16[64,512]{1,0:T(8,128)(2,1)} %fin_hbm.1, bf16[64,1792]{1,0:T(8,128)(2,1)} %fout_hbm.1, f32[8,4096]{1,0:T(8,128)} %query_ref.1, f32[64,64]{1,0:T(8,128)} %bin_ref.1, ...), custom_call_target="tpu_custom_call" | custom-call | tf_op jit(solution)/shard_map/pallas_call | solution.py:393
  60.5 1.5 %copy.10 = f32[128,8]{0,1:T(8,128)} copy(f32[128,8]{1,0:T(8,128)} %shard_map.91) | data formatting | bytes 8192 | tf_op jit(solution)/shard_map/pallas_call | solution.py:393

commit v3 on v2

--- a/solution.py
+++ b/solution.py
@@ -311,7 +311,7 @@
         ).astype(jnp.bfloat16)
 
     steps = len(route)
-    lead, lag, slow = 3, 3, 4
+    lead, lag, slow = 1, 4, 8
     order = []
     for k in range(steps + lead):
         if k < steps:
@@ -337,16 +337,16 @@
             cross(*order[i - lag])
         if i >= slow:
             close(*order[i - slow])
-    turn_rows(s)
-    for k in range(steps):
-        passed(2, k)
-        turn_rows(spot(k, c))
     for i in range(len(order), len(order) + slow):
         if i - lag < len(order):
             cross(*order[i - lag])
         close(*order[i - slow])
     rout[s] = acc_out[...].astype(jnp.bfloat16)
     spread(3)
+    turn_rows(s)
+    for k in range(steps):
+        passed(2, k)
+        turn_rows(spot(k, c))
     for k in range(-1, steps):
         p = dev_core[1] if k < 0 else spot(k, 1 - c)
         arrive(2, "all", p)

time: 62.2 us -> 53.9 us (0.87)
  Pallas kernels: 60.5 us -> 52.1 us
    pallas_call x1, Pallas kernels: 60.5 us -> 52.1 us  [in_one_kernel(): pl.pallas_call(functools.partial(kernel, n // 4), out_shape=jax.ShapeDtyp...]
where the time goes in v3:
time: 53.9 us; the launch traced here: 53.6 us
  Pallas kernels  52.1 us (97%)
  local copies, waits for them, and re-layouts  1.5 us (3%)
    pallas_call x1, Pallas kernels, in_one_kernel(): pl.pallas_call(functools.partial(kernel, n // 4), out_shape=jax.ShapeDtyp...  52.1 us
    pallas_call x1, local copies, waits for them, and re-layouts, in_one_kernel(): pl.pallas_call(functools.partial(kernel, n // 4), out_shape=jax.ShapeDtyp...  1.5 us

profile of v3, /device:TPU:0, one launch (start us, length us, event | category | flops | bytes accessed | tf_op | source)
XLA Modules:
  0.0 53.6 jit_solution(17528676414373686106)
XLA Ops:
  0.0 52.1 %shard_map.91 = f32[128,8]{1,0:T(8,128)} custom-call(bf16[128,8192]{1,0:T(8,128)(2,1)} %acts_hbm.1, bf16[128,28672]{1,0:T(8,128)(2,1)} %grads_hbm.1, s32[1,128]{1,0:T(1,128)} %ids_ref.1, bf16[64,512]{1,0:T(8,128)(2,1)} %fin_hbm.1, bf16[64,1792]{1,0:T(8,128)(2,1)} %fout_hbm.1, f32[8,4096]{1,0:T(8,128)} %query_ref.1, f32[64,64]{1,0:T(8,128)} %bin_ref.1, ...), custom_call_target="tpu_custom_call" | custom-call | tf_op jit(solution)/shard_map/pallas_call | solution.py:393
  52.1 1.5 %copy.10 = f32[128,8]{0,1:T(8,128)} copy(f32[128,8]{1,0:T(8,128)} %shard_map.91) | data formatting | bytes 8192 | tf_op jit(solution)/shard_map/pallas_call | solution.py:393

commit v4 on v3

--- a/solution.py
+++ b/solution.py
@@ -162,6 +162,8 @@
             return x, pl.multiple_of(x * quarter, quarter), quarter
         if g == "cross":
             return 1 - x, pl.multiple_of((1 - x) * quarter, quarter), quarter
+        if g == "whole":
+            return 3, 0, rank
         return 2, half, half
 
     def copy(f, g, p, kind, dev):
@@ -208,8 +210,7 @@
         for g in ("native", "rest"):
             along(f, g, s)
             send(f, g, s, 2, dev_y)
-        for g in ("native", "cross", "rest"):
-            send(f, g, s, 4, dev_core)
+        send(f, "whole", s, 4, dev_core)
 
     near = [
         sorted([w for w in range(lines) if w != v], key=lambda w: (abs(w - v), w))
@@ -246,7 +247,6 @@
                 send(f, g, p, 2, dev_y)
             if g == "native":
                 send(f, g, p, 3, dev_x)
-            send(f, g, p, 4, dev_core)
 
     def fold(f, p):
         xs, acc = ((acts, acc_in), (grads, acc_out))[f]
@@ -257,13 +257,12 @@
     def cross(f, k):
         p = spot(k, c)
         arrive(f, "cross", p)
-        send(f, "cross", p, 4, dev_core)
+        send(f, "whole", p, 4, dev_core)
         fold(f, p)
 
     def partner(f, k):
         p = dev_core[1] if k < 0 else spot(k, 1 - c)
-        for g in ("native", "cross", "rest"):
-            arrive(f, g, p)
+        arrive(f, "whole", p)
         fold(f, p)
 
     def turn_rows(p):
@@ -409,12 +408,12 @@
             pltpu.VMEM((rank, n_query, rank), f32),
             pltpu.VMEM((rank, n_query * rank), f32),
             dma((4,)),
-            dma((5, 3, n)),
-            dma((5, 3, n)),
+            dma((5, 4, n)),
+            dma((5, 4, n)),
             dma((n // 2, 1, n)),
             dma((n // 2, 1, n)),
-            dma((3, n)),
-            dma((3, n)),
+            dma((4, n)),
+            dma((4, n)),
             dma((1, n)),
             dma((1, n)),
         ],

time: 53.9 us -> 55.4 us (1.028)
  Pallas kernels: 52.1 us -> 53.7 us
    pallas_call x1, Pallas kernels: 52.1 us -> 53.7 us  [in_one_kernel(): pl.pallas_call(functools.partial(kernel, n // 4), out_shape=jax.ShapeDtyp...]
where the time goes in v4:
time: 55.4 us; the launch traced here: 55.2 us
  Pallas kernels  53.7 us (97%)
  local copies, waits for them, and re-layouts  1.5 us (3%)
    pallas_call x1, Pallas kernels, in_one_kernel(): pl.pallas_call(functools.partial(kernel, n // 4), out_shape=jax.ShapeDtyp...  53.7 us
    pallas_call x1, local copies, waits for them, and re-layouts, in_one_kernel(): pl.pallas_call(functools.partial(kernel, n // 4), out_shape=jax.ShapeDtyp...  1.5 us

profile of v4, /device:TPU:0, one launch (start us, length us, event | category | flops | bytes accessed | tf_op | source)
XLA Modules:
  0.0 55.2 jit_solution(27682966129479895)
XLA Ops:
  0.0 53.7 %shard_map.91 = f32[128,8]{1,0:T(8,128)} custom-call(bf16[128,8192]{1,0:T(8,128)(2,1)} %acts_hbm.1, bf16[128,28672]{1,0:T(8,128)(2,1)} %grads_hbm.1, s32[1,128]{1,0:T(1,128)} %ids_ref.1, bf16[64,512]{1,0:T(8,128)(2,1)} %fin_hbm.1, bf16[64,1792]{1,0:T(8,128)(2,1)} %fout_hbm.1, f32[8,4096]{1,0:T(8,128)} %query_ref.1, f32[64,64]{1,0:T(8,128)} %bin_ref.1, ...), custom_call_target="tpu_custom_call" | custom-call | tf_op jit(solution)/shard_map/pallas_call | solution.py:392
  53.7 1.5 %copy.10 = f32[128,8]{0,1:T(8,128)} copy(f32[128,8]{1,0:T(8,128)} %shard_map.91) | data formatting | bytes 8192 | tf_op jit(solution)/shard_map/pallas_call | solution.py:392

commit v5 on v3

--- a/solution.py
+++ b/solution.py
@@ -202,7 +202,7 @@
         send(f, g, p, 0, dev, cond)
 
     def yz_first(f, g):
-        return f == 0 and g == "rest"
+        return f == 1 and g == "rest"
 
     def own(f):
         for g in ("native", "rest"):

time: 53.9 us -> 53.7 us (level)
  no operation moved by 1% of the time
where the time goes in v5:
time: 53.7 us; the launch traced here: 53.5 us
  Pallas kernels  52 us (97%)
  local copies, waits for them, and re-layouts  1.5 us (3%)
    pallas_call x1, Pallas kernels, in_one_kernel(): pl.pallas_call(functools.partial(kernel, n // 4), out_shape=jax.ShapeDtyp...  52 us
    pallas_call x1, local copies, waits for them, and re-layouts, in_one_kernel(): pl.pallas_call(functools.partial(kernel, n // 4), out_shape=jax.ShapeDtyp...  1.5 us

profile of v5, /device:TPU:0, one launch (start us, length us, event | category | flops | bytes accessed | tf_op | source)
XLA Modules:
  0.0 53.5 jit_solution(15048750518106258801)
XLA Ops:
  0.0 52.0 %shard_map.91 = f32[128,8]{1,0:T(8,128)} custom-call(bf16[128,8192]{1,0:T(8,128)(2,1)} %acts_hbm.1, bf16[128,28672]{1,0:T(8,128)(2,1)} %grads_hbm.1, s32[1,128]{1,0:T(1,128)} %ids_ref.1, bf16[64,512]{1,0:T(8,128)(2,1)} %fin_hbm.1, bf16[64,1792]{1,0:T(8,128)(2,1)} %fout_hbm.1, f32[8,4096]{1,0:T(8,128)} %query_ref.1, f32[64,64]{1,0:T(8,128)} %bin_ref.1, ...), custom_call_target="tpu_custom_call" | custom-call | tf_op jit(solution)/shard_map/pallas_call | solution.py:393
  52.0 1.5 %copy.10 = f32[128,8]{0,1:T(8,128)} copy(f32[128,8]{1,0:T(8,128)} %shard_map.91) | data formatting | bytes 8192 | tf_op jit(solution)/shard_map/pallas_call | solution.py:393
